TPU v7x, 128 devices: a whole 4x4x4 slice. The times are simulated.
128 devices in a mesh: dom: 16 (over y_hi, z, core), blk: 8 (over x, y_lo).
Axes of the slice: x: 4, y: 4 (y_hi: 2, y_lo: 2; y = y_hi * 2 + y_lo), z: 4, core: 2. Of those that a mesh axis runs over, the one named last changes fastest.
Arguments:
- images: bfloat16 [1024, 128, 256], P('dom', 'blk'), may hold values from -4.5 to 6.5
- ref_store: bfloat16 [16, 16, 4, 128, 256], P('dom', None, None, 'blk'), may hold values from -0.03125 to 0.03125
- block_owner: int32 [16], replicated, may hold values from 0 to 15, as said below
- class_gain: float32 [64], replicated, may hold values from 0.5 to 2
- precision: float32 [1024], P('dom'), may hold values from 0.5 to 80
Outputs:
- class_sums: float32 [16, 1, 4, 128, 256], P('dom', None, None, 'blk')
Inputs may be any that keep to these rules, and one draw needn't show every extreme that they name: `block_owner`: each index d of dom owns exactly 1 block.
All inputs are finite; a program needn't handle non-finite values.
Results may differ from a plain program's by a relative error of at most 0.0049.
Values may be sent and summed in bfloat16 or wider, within the bound.
No kernel may reach another device: no remote copies, remote signals or barrier semaphores. Data moves between devices by JAX's collectives and lax.ppermute only.
A program may use at most 64 MiB of HBM per device.

v0:
```python
import jax
import jax.numpy as jnp
from jax import lax
from jax.experimental import pallas as pl
from jax.experimental.pallas import tpu as pltpu
from jax.sharding import Mesh, PartitionSpec as P


BF = jnp.bfloat16
F32 = jnp.float32
VM = pltpu.VMEM
LANES = 128
N1 = 4
N2 = 8
PARTNERS = (0, 1, 3, 2)


def spec(space=VM):
    return pl.BlockSpec(memory_space=space)


def params(mib=24):
    return pltpu.CompilerParams(vmem_limit_bytes=mib * 1024 * 1024)


def here(x):
    return pltpu.with_memory_space_constraint(x, VM)


def away(x):
    return pltpu.with_memory_space_constraint(x, pltpu.HBM)


def fill(scr, value):
    for h in range(scr.shape[0]):
        scr[h] = value[:, h * LANES : (h + 1) * LANES]


def take_cycle(scr, r, rows, cycles):
    return [scr.at[h][pl.ds(r, rows, stride=cycles), :] for h in range(2)]


def narrow(x):
    wide = x * 65537.0
    return wide - (wide - x)


def narrow_sum(x):
    near = narrow(x)
    lane = lax.broadcasted_iota(jnp.int32, x.shape, 1)
    rest = jnp.sum(x - near, axis=1, keepdims=True)
    return jnp.where(lane == 0, near + rest, near)


def turn(plus, minus, t):
    t = t % (2 * LANES)
    if t == 0:
        return plus, minus
    if t >= LANES:
        return turn(plus, -minus, t - LANES)
    lane = lax.broadcasted_iota(jnp.int32, minus.shape, 1)
    minus = pltpu.roll(minus, t, 1)
    return pltpu.roll(plus, t, 1), jnp.where(lane < t, -minus, minus)


def pick_block(me, nb, block_owner, class_gain, ref_store):
    nblk, kb, cycles, angles = ref_store.shape

    def body(me_ref, owner_ref, gain_ref, store_ref, out_ref):
        block = jnp.int32(0)
        for b in range(nblk):
            block = jnp.where(owner_ref[b] == me_ref[0] // nb, jnp.int32(b), block)
        for i in range(kb):
            piece = (store_ref[block, i].astype(F32) * gain_ref[block * kb + i]).astype(BF).astype(F32)
            a, b = piece[:, :LANES], piece[:, LANES:]
            piece = jnp.concatenate([narrow_sum(a + b), narrow(a - b)], axis=1).astype(BF)
            out_ref[i * cycles : (i + 1) * cycles, :] = piece

    return pl.pallas_call(
        body,
        out_shape=VM((kb * cycles, angles), BF),
        in_specs=[spec(pltpu.SMEM), spec(pltpu.SMEM), spec(pltpu.SMEM), spec()],
        out_specs=spec(),
        compiler_params=params(60),
        name="pick_block",
    )(me, block_owner, class_gain, away(ref_store))


def halve_images(own, other, nb):
    particles, cycles, angles = own.shape
    per = particles // nb

    def body(own_hbm, other_ref, out_ref, a_scr, b_scr, own_ref, sem):
        copy = pltpu.make_async_copy(own_hbm, own_ref, sem)
        copy.start()
        fill(b_scr, other_ref[...].astype(F32).reshape(particles * cycles, angles))
        copy.wait()
        fill(a_scr, own_ref[...].astype(F32).reshape(particles * cycles, angles))
        for r in range(cycles):
            a = take_cycle(a_scr, r, particles, cycles)
            b = take_cycle(b_scr, r, particles, cycles)
            for i, op in enumerate((jnp.add, jnp.subtract)):
                x, y = op(a[0], a[1]), op(b[0], b[1])
                both = [v.reshape(nb, per, LANES) for v in (x, y)]
                both = jnp.concatenate(both, axis=1).reshape(2 * particles, LANES)
                out_ref[i, r] = narrow(both).astype(BF)

    return pl.pallas_call(
        body,
        out_shape=VM((2, cycles, 2 * particles, LANES), BF),
        in_specs=[spec(pltpu.HBM), spec()],
        out_specs=spec(),
        scratch_shapes=[VM((2, particles * cycles, LANES), F32)] * 2
        + [VM(own.shape, BF), pltpu.SemaphoreType.DMA],
        compiler_params=params(),
        name="halve_images",
    )(away(own), here(other))


def pair_up(mine, theirs, *others):
    def body(a_ref, b_ref, *refs):
        out_ref = refs[-1]
        out_ref[0] = a_ref[...]
        out_ref[1] = b_ref[...]

    return pl.pallas_call(
        body,
        out_shape=VM((2,) + mine.shape, BF),
        in_specs=[spec()] * (2 + len(others)),
        out_specs=spec(),
        compiler_params=params(),
        name="pair_up",
    )(here(mine), here(theirs), *[here(o) for o in others])


def rotate_images(x_ref, r, nb, step):
    plus, minus = x_ref[0, r], x_ref[1, r]
    per = plus.shape[0] // nb
    turned = [turn(plus, minus, step * s) for s in range(N1)]
    return [
        jnp.concatenate(
            [t[i][j * per : (j + 1) * per] for j in range(nb) for t in turned], axis=0
        )
        for i in range(2)
    ]


def turn_images(images, nb, step):
    _, cycles, particles, _ = images.shape

    def body(x_ref, out_ref):
        for r in range(cycles):
            out_ref[0, r], out_ref[1, r] = rotate_images(x_ref, r, nb, step)

    return pl.pallas_call(
        body,
        out_shape=VM((2, cycles, N1 * particles, LANES), BF),
        in_specs=[spec()],
        out_specs=spec(),
        compiler_params=params(),
        name="turn_images",
    )(here(images))


def correlate(turned, refs, nb, step, before=()):
    _, cycles, total, _ = turned.shape
    rows = total // nb
    near, far = refs[0].shape[:2]
    classes = len(refs) * near * far // cycles
    cols = N2 * classes
    angles = 2 * LANES
    tiles = 1 + len(before)

    def body(x_ref, *args):
        r_refs, (out_ref, scr, rr) = args[: len(refs)], args[-3:]
        for t, b_ref in enumerate(args[len(refs) : -3]):
            out_ref[:, t] = b_ref[:, 0]
        blocks = [r_ref[d].astype(F32) for r_ref in r_refs for d in range(near)]
        fill(scr, jnp.concatenate(blocks, axis=0))
        square = jnp.zeros((classes, LANES), F32)
        for r in range(cycles):
            plus, minus = take_cycle(scr, r, classes, cycles)
            square = square + 0.5 * (plus * plus + minus * minus)
            plus, minus = plus.astype(BF), minus.astype(BF)
            for s in range(N2):
                p, m = turn(plus, minus, angles - step * N1 * s)
                rr[0, r, s * classes : (s + 1) * classes, :] = p
                rr[1, r, s * classes : (s + 1) * classes, :] = m
        norm = jnp.broadcast_to(jnp.sum(square, axis=1, keepdims=True), (classes, cols))
        k = lax.broadcasted_iota(jnp.int32, (classes, cols), 0)
        lane = lax.broadcasted_iota(jnp.int32, (classes, cols), 1)
        norm = jnp.sum(jnp.where(lane % classes == k, norm, 0.0), axis=0, keepdims=True)
        for i in range(2):
            left = jnp.concatenate([x_ref[i, r] for r in range(cycles)], axis=1)
            right = jnp.concatenate([rr[i, r] for r in range(cycles)], axis=1)
            part = lax.dot_general(
                left, right, (((1,), (1,)), ((), ())), preferred_element_type=F32
            )
            if i == 0:
                part = part - norm
            at = slice(i * rows, (i + 1) * rows)
            out_ref[:, tiles - 1, at, :] = part.astype(BF).reshape(nb, rows, LANES)

    return pl.pallas_call(
        body,
        out_shape=VM((nb, tiles, 2 * rows, LANES), BF),
        in_specs=[spec()] * (len(refs) + tiles),
        out_specs=spec(),
        scratch_shapes=[
            VM((2, classes * cycles, LANES), F32),
            VM((2, cycles, cols, LANES), BF),
        ],
        compiler_params=params(),
        name="correlate",
    )(here(turned), *[here(r) for r in (*refs, *before)])


def local_softmax(me, scores, precision, others):
    nb, tiles, rows, _ = scores.shape
    cols = tiles * LANES
    half = rows // 2
    group = half // N1
    own = group // 2

    def across(op, x):
        pieces = [x[i * group : (i + 1) * group] for i in range(N1)]
        return op(op(pieces[0], pieces[1]), op(pieces[2], pieces[3]))

    def body(me_ref, x_ref, a_ref, b_ref, e_ref, stat_ref):
        total = x_ref[0].astype(F32)
        for i in range(1, nb):
            total = total + x_ref[i].astype(F32)
        total = jnp.concatenate([total[t] for t in range(tiles)], axis=1)
        plus, minus = total[:half], total[half:]
        wide = (own, nb * own)
        row = lax.broadcasted_iota(jnp.int32, wide, 0) + me_ref[0] % nb * own
        mine = row == lax.broadcasted_iota(jnp.int32, wide, 1)
        scale = [
            jnp.sum(jnp.where(mine, ref[...], 0.0), axis=1, keepdims=True)
            for ref in (a_ref, b_ref)
        ]
        scale = jnp.concatenate(scale * N1, axis=0) * 0.5
        near, far = scale * (plus + minus), scale * (plus - minus)
        top = jnp.max(jnp.maximum(near, far), axis=1, keepdims=True)
        top = across(jnp.maximum, top)
        tops = jnp.concatenate([top] * N1, axis=0)
        near, far = jnp.exp(near - tops), jnp.exp(far - tops)
        e_ref[0] = near
        e_ref[1] = far
        amount = across(jnp.add, jnp.sum(near + far, axis=1, keepdims=True))
        stat_ref[0] = jnp.broadcast_to(top, (group, LANES))
        stat_ref[1] = jnp.broadcast_to(amount, (group, LANES))

    return pl.pallas_call(
        body,
        out_shape=(VM((2, half, cols), F32), VM((2, group, LANES), F32)),
        in_specs=[spec(pltpu.SMEM), spec(), spec(), spec()],
        out_specs=(spec(), spec()),
        compiler_params=params(),
        name="local_softmax",
    )(me, here(scores), here(precision), here(others))


def normalize(e, mine, theirs, copies):
    _, half, cols = e.shape
    group = mine.shape[1]

    def body(e_ref, a_ref, b_ref, out_ref):
        def flipped(x):
            return jnp.concatenate([x[group // 2 :], x[: group // 2]], axis=0)

        top_a, sum_a = a_ref[0], a_ref[1]
        top_b, sum_b = flipped(b_ref[0]), flipped(b_ref[1])
        top = jnp.maximum(top_a, top_b)
        part = jnp.exp(top_a - top)
        factor = part / (sum_a * part + sum_b * jnp.exp(top_b - top))
        factor = jnp.concatenate([jnp.concatenate([factor] * N1, axis=0)] * (cols // LANES), axis=1)
        near, far = e_ref[0] * factor, e_ref[1] * factor
        w = jnp.concatenate([near + far, near - far], axis=0).T.astype(BF)
        for c in range(copies):
            out_ref[c] = w

    return pl.pallas_call(
        body,
        out_shape=VM((copies, cols, 2 * half), BF),
        in_specs=[spec(), spec(), spec()],
        out_specs=spec(),
        compiler_params=params(),
        name="normalize",
    )(here(e), here(mine), here(theirs))


def accumulate(me, weights, turned, ny, nz, step):
    owners = ny * nz
    nb, cols, lanes = weights.shape
    cycles = turned.shape[1]
    classes = cols // N2
    per = LANES // N2
    pair = 2 * LANES

    def body(me_ref, w_ref, x_ref, out_ref, scr):
        left = lax.broadcasted_iota(jnp.int32, (cols, lanes), 1) < lanes // 2
        near, far = [], []
        for j in range(0, nb, 2):
            a, b = w_ref[j], w_ref[j + 1]
            near.append(jnp.where(left, a, pltpu.roll(b, lanes // 2, 1)))
            far.append(jnp.where(left, pltpu.roll(a, lanes // 2, 1), b))
        w = [jnp.concatenate(v, axis=1) for v in (near, far)]
        for c in range(0, cycles, 2):
            spread = []
            for i in range(2):
                both = jnp.concatenate([x_ref[i, c], x_ref[i, c + 1]], axis=1)
                spread.append(jnp.dot(w[i], both, preferred_element_type=F32))
            for d in range(2):
                plus = minus = None
                for s in range(N2):
                    p, m = (
                        jnp.concatenate(
                            [
                                v[t + s * per : t + (s + 1) * per, d * LANES : (d + 1) * LANES]
                                for t in range(0, cols, LANES)
                            ],
                            axis=0,
                        )
                        for v in spread
                    )
                    p, m = turn(p, m, step * N1 * s)
                    plus = plus + p if s else p
                    minus = minus + m if s else m
                rows = pl.ds(c + d, classes, stride=cycles)
                scr.at[0][rows, :] = 0.5 * (plus + minus)
                scr.at[1][rows, :] = 0.5 * (plus - minus)
        whole = jnp.concatenate([scr[0], scr[1]], axis=1)
        whole = whole.reshape(out_ref.shape).astype(BF)
        place = me_ref[0] // (2 * nb)
        y, z = place // nz, place % nz
        for slot in range(owners):
            dz, dy = PARTNERS[slot // ny], slot % ny
            out_ref[(y ^ dy) * nz + (z ^ dz)] = whole[slot]

    return pl.pallas_call(
        body,
        out_shape=VM((owners, classes // owners * cycles, pair), BF),
        in_specs=[spec(pltpu.SMEM), spec(), spec()],
        out_specs=spec(),
        scratch_shapes=[
            VM((2, classes * cycles, LANES), F32),
        ],
        compiler_params=params(),
        name="accumulate",
    )(me, here(weights), here(turned))


def add_up(parts):
    def body(x_ref, out_ref):
        total = x_ref[0].astype(F32)
        for i in range(1, parts.shape[0]):
            total = total + x_ref[i].astype(F32)
        out_ref[...] = total

    return pl.pallas_call(
        body,
        out_shape=jax.ShapeDtypeStruct(parts.shape[1:], F32),
        in_specs=[spec()],
        out_specs=spec(),
        compiler_params=params(),
        name="add_up",
    )(here(parts))


def solution(mesh):
    dom, nb = mesh.devices.shape
    ny, nz = 2, dom // 4
    view = Mesh(mesh.devices.reshape(ny, nz, 2, nb), ("yh", "z", "core", "blk"))
    swap = [(0, 1), (1, 0)]

    def shards(images, ref_store, block_owner, class_gain, precision):
        particles, cycles, angles = images.shape
        kb = ref_store.shape[2]
        rot = angles // (2 * N1 * N2)
        other = lax.ppermute(images, "core", swap)
        other_precision = lax.ppermute(precision, "core", swap)
        y, z = lax.axis_index("yh"), lax.axis_index("z")
        me = ((y * nz + z) * 2 + lax.axis_index("core")) * nb + lax.axis_index("blk")
        me = me[None].astype(jnp.int32)
        mine = pick_block(me, nb, block_owner, class_gain, ref_store[0])
        theirs = lax.ppermute(mine, "yh", swap)
        halves = halve_images(images, other, nb)
        refs = [pair_up(mine, theirs, halves, other_precision)]
        for d in PARTNERS[1:]:
            ring = [(i, i ^ d) for i in range(nz)]
            refs.append(lax.ppermute(refs[0], "z", ring))
        turned = turn_images(halves, nb, rot)
        early = correlate(turned, refs[:2], nb, rot)
        scores = correlate(turned, refs[2:], nb, rot, (early,))
        scores = lax.all_to_all(scores, "blk", 0, 0)
        flat = (1, particles)
        e, stats = local_softmax(
            me, scores, precision.reshape(flat), other_precision.reshape(flat)
        )
        theirs = lax.ppermute(stats, "core", swap)
        weights = normalize(e, stats, theirs, nb)
        weights = lax.all_to_all(weights, "blk", 0, 0)
        totals = accumulate(me, weights, turned, ny, nz, rot)
        totals = lax.all_to_all(totals, ("yh", "z"), 0, 0)
        return add_up(totals).reshape(1, 1, kb, cycles, angles)

    dom_axes = ("yh", "z", "core")
    return jax.shard_map(
        shards,
        mesh=view,
        in_specs=(
            P(dom_axes, "blk", None),
            P(dom_axes, None, None, "blk", None),
            P(),
            P(),
            P(dom_axes),
        ),
        out_specs=P(dom_axes, None, None, "blk", None),
        check_vma=False,
    )
```

profile of v0, /device:TPU:0, one launch (start us, length us, event | category | flops | bytes accessed | tf_op | source)
XLA Modules:
  0.0 62.1 jit_solution(12837575866865172509)
XLA Ops:
  0.0 0.0 collective-permute-start
  0.0 1.2 %pick_block.1.a_ref = bf16[64,256]{1,0:T(8,128)(2,1)S(1)} custom-call(s32[1]{0:T(128)} %bitcast.me_ref, s32[16]{0:T(128)} %owner_ref.1, f32[64]{0:T(128)} %gain_ref.1, bf16[16,4,16,256]{3,2,1,0:T(8,128)(2,1)} %bitcast.7), custom_call_target="tpu_custom_call" | custom-call | tf_op jit(solution)/shard_map/pick_block/pallas_call | solution.py:79
  1.2 3.4 %collective-permute-start.1 = (bf16[64,256]{1,0:T(8,128)(2,1)S(1)}, bf16[64,256]{1,0:T(8,128)(2,1)S(1)}, u32[]{:S(2)}, u32[]{:S(2)}) collective-permute-start(bf16[64,256]{1,0:T(8,128)(2,1)S(1)} %pick_block.1.a_ref), channel_id=1, source_target_pairs={{0,64},{64,0},{1,65},{65,1},{2,66},{66,2},{3,67},{67,3},{4,68},{68... | collective-permute-start | bytes 98312 | tf_op jit(solution)/shard_map/ppermute | solution.py:387
  4.6 0.2 collective-permute-start.2
  4.8 0.0 collective-permute-done.other_ref
  4.8 2.3 %halve_images.1.x_ref.refs_0_ = bf16[2,16,128,128]{3,2,1,0:T(8,128)(2,1)S(1)} custom-call(bf16[64,16,256]{2,1,0:T(8,128)(2,1)} %own_hbm.1, bf16[64,16,256]{2,1,0:T(8,128)(2,1)S(1)} %collective-permute-done.other_ref), custom_call_target="tpu_custom_call" | custom-call | tf_op jit(solution)/shard_map/halve_images/pallas_call | solution.py:108
  7.1 0.0 collective-permute-done.2.refs_1_
  7.1 0.0 collective-permute-done.1.b_ref
  7.1 2.0 %collective-permute-start.5 = (bf16[2,64,256]{2,1,0:T(8,128)(2,1)S(1)}, bf16[2,64,256]{2,1,0:T(8,128)(2,1)S(1)}, u32[]{:S(2)}, u32[]{:S(2)}) collective-permute-start(bf16[2,64,256]{2,1,0:T(8,128)(2,1)S(1)} %pair_up.1.args_0_), channel_id=1, source_target_pairs={{0,16},{16,0},{32,48},{48,32},{1,17},{17,1},{33,49},{49,33},{2,18}... | collective-permute-start | bytes 196616 | tf_op jit(solution)/shard_map/ppermute | solution.py:392
  9.1 2.5 %collective-permute-start.3 = (bf16[2,64,256]{2,1,0:T(8,128)(2,1)S(1)}, bf16[2,64,256]{2,1,0:T(8,128)(2,1)S(1)}, u32[]{:S(2)}, u32[]{:S(2)}) collective-permute-start(bf16[2,64,256]{2,1,0:T(8,128)(2,1)S(1)} %pair_up.1.args_0_), channel_id=1, source_target_pairs={{0,48},{16,32},{32,16},{48,0},{1,49},{17,33},{33,17},{49,1},{2,50}... | collective-permute-start | bytes 196616 | tf_op jit(solution)/shard_map/ppermute | solution.py:392
  11.7 1.1 %collective-permute-start.4 = (bf16[2,64,256]{2,1,0:T(8,128)(2,1)S(1)}, bf16[2,64,256]{2,1,0:T(8,128)(2,1)S(1)}, u32[]{:S(2)}, u32[]{:S(2)}) collective-permute-start(bf16[2,64,256]{2,1,0:T(8,128)(2,1)S(1)} %pair_up.1.args_0_), channel_id=1, source_target_pairs={{0,32},{16,48},{32,0},{48,16},{1,33},{17,49},{33,1},{49,17},{2,34}... | collective-permute-start | bytes 196616 | tf_op jit(solution)/shard_map/ppermute | solution.py:392
  12.7 0.9 %turn_images.1.x_ref = bf16[2,16,512,128]{3,2,1,0:T(8,128)(2,1)S(1)} custom-call(bf16[2,16,128,128]{3,2,1,0:T(8,128)(2,1)S(1)} %halve_images.1.x_ref.refs_0_), custom_call_target="tpu_custom_call" | custom-call | tf_op jit(solution)/shard_map/turn_images/pallas_call | solution.py:155
  13.6 0.0 collective-permute-done.5.args_1_
  13.6 1.4 %correlate.2.args_2_ = bf16[8,1,128,128]{3,2,1,0:T(8,128)(2,1)S(1)} custom-call(bf16[2,16,512,128]{3,2,1,0:T(8,128)(2,1)S(1)} %turn_images.1.x_ref, bf16[2,64,256]{2,1,0:T(8,128)(2,1)S(1)} %pair_up.1.args_0_, bf16[2,64,256]{2,1,0:T(8,128)(2,1)S(1)} %collective-permute-done.5.args_1_), custom_call_target="tpu_custom_call" | custom-call | tf_op jit(solution)/shard_map/correlate/pallas_call | solution.py:204
  15.0 0.0 copy-start
  15.0 0.0 collective-permute-done.3.args_0_
  15.0 2.4 %collective-permute-done.4.args_1_ = bf16[2,64,256]{2,1,0:T(8,128)(2,1)S(1)} collective-permute-done((bf16[2,64,256]{2,1,0:T(8,128)(2,1)S(1)}, bf16[2,64,256]{2,1,0:T(8,128)(2,1)S(1)}, u32[]{:S(2)}, u32[]{:S(2)}) %collective-permute-start.4) | collective-permute-done | bytes 65568 | tf_op jit(solution)/shard_map/ppermute | solution.py:392
  17.4 1.4 %correlate.3 = bf16[8,2,128,128]{3,2,1,0:T(8,128)(2,1)S(1)} custom-call(bf16[2,16,512,128]{3,2,1,0:T(8,128)(2,1)S(1)} %turn_images.1.x_ref, bf16[2,64,256]{2,1,0:T(8,128)(2,1)S(1)} %collective-permute-done.3.args_0_, bf16[2,64,256]{2,1,0:T(8,128)(2,1)S(1)} %collective-permute-done.4.args_1_, bf16[8,1,128,128]{3,2,1,0:T(8,128)(2,1)S(1)} %correlate.2.args_2_), custom_call_target="tpu_custom_call" | custom-call | tf_op jit(solution)/shard_map/correlate/pallas_call | solution.py:204
  18.8 13.0 %all_to_all.15.x_ref = bf16[8,2,128,128]{3,2,1,0:T(8,128)(2,1)S(1)} all-to-all(bf16[8,2,128,128]{3,2,1,0:T(8,128)(2,1)S(1)} %correlate.3), channel_id=1, replica_groups=mesh['yh'=2,'z'=4,'core'=2,'blk'=8] {'blk'}, dimensions={0} | all-to-all | bytes 1048576 | tf_op jit(solution)/shard_map/all_to_all | solution.py:396
  31.9 0.0 copy-done
  31.9 0.4 local_softmax.1
  32.3 0.1 collective-permute-start.6
  32.3 1.2 %collective-permute-done.6.b_ref = f32[2,16,128]{2,1,0:T(8,128)S(1)} collective-permute-done((f32[2,16,128]{2,1,0:T(8,128)S(1)}, f32[2,16,128]{2,1,0:T(8,128)S(1)}, u32[]{:S(2)}, u32[]{:S(2)}) %collective-permute-start.6) | collective-permute-done | bytes 16416 | tf_op jit(solution)/shard_map/ppermute | solution.py:401
  33.5 0.1 normalize.1
  33.7 12.9 %all_to_all.16.w_ref = bf16[8,256,128]{2,1,0:T(8,128)(2,1)S(1)} all-to-all(bf16[8,256,128]{2,1,0:T(8,128)(2,1)S(1)} %normalize.1), channel_id=1, replica_groups=mesh['yh'=2,'z'=4,'core'=2,'blk'=8] {'blk'}, dimensions={0} | all-to-all | bytes 1048576 | tf_op jit(solution)/shard_map/all_to_all | solution.py:403
  46.6 1.6 %accumulate.1 = bf16[8,64,256]{2,1,0:T(8,128)(2,1)S(1)} custom-call(s32[1]{0:T(128)} %bitcast.me_ref, bf16[8,256,128]{2,1,0:T(8,128)(2,1)S(1)} %all_to_all.16.w_ref, bf16[2,16,512,128]{3,2,1,0:T(8,128)(2,1)S(1)} %turn_images.1.x_ref), custom_call_target="tpu_custom_call" | custom-call | tf_op jit(solution)/shard_map/accumulate/pallas_call | solution.py:341
  48.3 13.2 %all_to_all.17.x_ref = bf16[8,64,256]{2,1,0:T(8,128)(2,1)S(1)} all-to-all(bf16[8,64,256]{2,1,0:T(8,128)(2,1)S(1)} %accumulate.1), channel_id=1, replica_groups=mesh['yh'=2,'z'=4,'core'=2,'blk'=8] {'yh','z'}, dimensions={0} | all-to-all | bytes 524288 | tf_op jit(solution)/shard_map/all_to_all | solution.py:405
  61.5 0.7 %add_up.1 = f32[64,256]{1,0:T(8,128)} custom-call(bf16[8,64,256]{2,1,0:T(8,128)(2,1)S(1)} %all_to_all.17.x_ref), custom_call_target="tpu_custom_call" | custom-call | tf_op jit(solution)/shard_map/add_up/pallas_call | solution.py:361
  (1 shorter events, 0.0 us)
Async XLA Ops:
  0.0 4.8 %collective-permute-start = (bf16[64,16,256]{2,1,0:T(8,128)(2,1)}, bf16[64,16,256]{2,1,0:T(8,128)(2,1)S(1)}, u32[]{:S(2)}, u32[]{:S(2)}) collective-permute-start(bf16[64,16,256]{2,1,0:T(8,128)(2,1)} %own_hbm.1), channel_id=1, source_target_pairs={{0,8},{8,0},{1,9},{9,1},{2,10},{10,2},{3,11},{11,3},{4,12},{12,4},... | collective-permute-start | bytes 1572872 | tf_op jit(solution)/shard_map/ppermute | solution.py:381
  1.2 5.9 %collective-permute-start.1 = (bf16[64,256]{1,0:T(8,128)(2,1)S(1)}, bf16[64,256]{1,0:T(8,128)(2,1)S(1)}, u32[]{:S(2)}, u32[]{:S(2)}) collective-permute-start(bf16[64,256]{1,0:T(8,128)(2,1)S(1)} %pick_block.1.a_ref), channel_id=1, source_target_pairs={{0,64},{64,0},{1,65},{65,1},{2,66},{66,2},{3,67},{67,3},{4,68},{68... | collective-permute-start | bytes 98312 | tf_op jit(solution)/shard_map/ppermute | solution.py:387
  4.6 2.5 %collective-permute-start.2 = (f32[64]{0:T(128)}, f32[64]{0:T(128)S(1)}, u32[]{:S(2)}, u32[]{:S(2)}) collective-permute-start(f32[64]{0:T(128)} %param.9), channel_id=1, source_target_pairs={{0,8},{8,0},{1,9},{9,1},{2,10},{10,2},{3,11},{11,3},{4,12},{12,4},... | collective-permute-start | bytes 776 | tf_op jit(solution)/shard_map/ppermute | solution.py:382
  7.1 6.5 %collective-permute-start.5 = (bf16[2,64,256]{2,1,0:T(8,128)(2,1)S(1)}, bf16[2,64,256]{2,1,0:T(8,128)(2,1)S(1)}, u32[]{:S(2)}, u32[]{:S(2)}) collective-permute-start(bf16[2,64,256]{2,1,0:T(8,128)(2,1)S(1)} %pair_up.1.args_0_), channel_id=1, source_target_pairs={{0,16},{16,0},{32,48},{48,32},{1,17},{17,1},{33,49},{49,33},{2,18}... | collective-permute-start | bytes 196616 | tf_op jit(solution)/shard_map/ppermute | solution.py:392
  9.1 5.9 %collective-permute-start.3 = (bf16[2,64,256]{2,1,0:T(8,128)(2,1)S(1)}, bf16[2,64,256]{2,1,0:T(8,128)(2,1)S(1)}, u32[]{:S(2)}, u32[]{:S(2)}) collective-permute-start(bf16[2,64,256]{2,1,0:T(8,128)(2,1)S(1)} %pair_up.1.args_0_), channel_id=1, source_target_pairs={{0,48},{16,32},{32,16},{48,0},{1,49},{17,33},{33,17},{49,1},{2,50}... | collective-permute-start | bytes 196616 | tf_op jit(solution)/shard_map/ppermute | solution.py:392
  11.7 5.8 %collective-permute-start.4 = (bf16[2,64,256]{2,1,0:T(8,128)(2,1)S(1)}, bf16[2,64,256]{2,1,0:T(8,128)(2,1)S(1)}, u32[]{:S(2)}, u32[]{:S(2)}) collective-permute-start(bf16[2,64,256]{2,1,0:T(8,128)(2,1)S(1)} %pair_up.1.args_0_), channel_id=1, source_target_pairs={{0,32},{16,48},{32,0},{48,16},{1,33},{17,49},{33,1},{49,17},{2,34}... | collective-permute-start | bytes 196616 | tf_op jit(solution)/shard_map/ppermute | solution.py:392
  15.0 16.8 %copy-start = (f32[64]{0:T(128)S(1)}, f32[64]{0:T(128)}, u32[]{:S(2)}) copy-start(f32[64]{0:T(128)} %param.9) | copy-start | bytes 772
  32.3 1.2 %collective-permute-start.6 = (f32[2,16,128]{2,1,0:T(8,128)S(1)}, f32[2,16,128]{2,1,0:T(8,128)S(1)}, u32[]{:S(2)}, u32[]{:S(2)}) collective-permute-start(f32[2,16,128]{2,1,0:T(8,128)S(1)} %get-tuple-element.8.a_ref), channel_id=1, source_target_pairs={{0,8},{8,0},{1,9},{9,1},{2,10},{10,2},{3,11},{11,3},{4,12},{12,4},... | collective-permute-start | bytes 49160 | tf_op jit(solution)/shard_map/ppermute | solution.py:401
where the time goes:
time: 62.4 us; the launch traced here: 62.1 us
  blocking collectives  39.2 us (63%)
  Pallas kernels  10 us (16%)
  starting transfers between devices  9.25 us (15%)
  waiting for transfers between devices  3.56 us (6%)
    all_to_all x1, blocking collectives, shards(): totals = lax.all_to_all(totals, ('yh', 'z'), 0, 0)  13.2 us
    all_to_all x1, blocking collectives, shards(): scores = lax.all_to_all(scores, 'blk', 0, 0)  13 us
    all_to_all x1, blocking collectives, shards(): weights = lax.all_to_all(weights, 'blk', 0, 0)  12.9 us
    ppermute x3, starting transfers between devices, shards(): refs.append(lax.ppermute(refs[0], 'z', ring))  5.58 us
    ppermute x1, starting transfers between devices, shards(): theirs = lax.ppermute(mine, 'yh', swap)  3.39 us
    pallas_call x2, Pallas kernels, correlate(): pl.pallas_call(body, out_shape=VM((nb, tiles, 2 * rows, LANES), BF), in_s...  2.81 us
    ppermute x3, waiting for transfers between devices, shards(): refs.append(lax.ppermute(refs[0], 'z', ring))  2.38 us
    pallas_call x1, Pallas kernels, halve_images(): pl.pallas_call(body, out_shape=VM((2, cycles, 2 * particles, LANES), BF),...  2.3 us
  transfers between devices with their start and end apart: 7, of which 2 were waited for; matrix products, arithmetic and copies ran while one was open for 0% of the time, Pallas kernels for 9%

commit v1 on v0

--- a/solution.py
+++ b/solution.py
@@ -93,17 +93,18 @@
     def body(own_hbm, other_ref, out_ref, a_scr, b_scr, own_ref, sem):
         copy = pltpu.make_async_copy(own_hbm, own_ref, sem)
         copy.start()
-        fill(b_scr, other_ref[...].astype(F32).reshape(particles * cycles, angles))
-        copy.wait()
-        fill(a_scr, own_ref[...].astype(F32).reshape(particles * cycles, angles))
-        for r in range(cycles):
-            a = take_cycle(a_scr, r, particles, cycles)
-            b = take_cycle(b_scr, r, particles, cycles)
-            for i, op in enumerate((jnp.add, jnp.subtract)):
-                x, y = op(a[0], a[1]), op(b[0], b[1])
-                both = [v.reshape(nb, per, LANES) for v in (x, y)]
-                both = jnp.concatenate(both, axis=1).reshape(2 * particles, LANES)
-                out_ref[i, r] = narrow(both).astype(BF)
+        for h, ref, scr in ((1, other_ref, b_scr), (0, own_ref, a_scr)):
+            if h == 0:
+                copy.wait()
+            fill(scr, ref[...].astype(F32).reshape(particles * cycles, angles))
+            for r in range(cycles):
+                a, b = take_cycle(scr, r, particles, cycles)
+                for i, v in enumerate((a + b, a - b)):
+                    v = narrow(v)
+                    for j in range(nb):
+                        at = (2 * j + h) * per
+                        piece = v[j * per : (j + 1) * per]
+                        out_ref[i, r, at : at + per, :] = piece.astype(BF)
 
     return pl.pallas_call(
         body,
@@ -172,8 +173,8 @@
     tiles = 1 + len(before)
 
     def body(x_ref, *args):
-        r_refs, (out_ref, scr, rr) = args[: len(refs)], args[-3:]
-        for t, b_ref in enumerate(args[len(refs) : -3]):
+        r_refs, (out_ref, scr) = args[: len(refs)], args[-2:]
+        for t, b_ref in enumerate(args[len(refs) : -2]):
             out_ref[:, t] = b_ref[:, 0]
         blocks = [r_ref[d].astype(F32) for r_ref in r_refs for d in range(near)]
         fill(scr, jnp.concatenate(blocks, axis=0))
@@ -181,18 +182,18 @@
         for r in range(cycles):
             plus, minus = take_cycle(scr, r, classes, cycles)
             square = square + 0.5 * (plus * plus + minus * minus)
-            plus, minus = plus.astype(BF), minus.astype(BF)
-            for s in range(N2):
-                p, m = turn(plus, minus, angles - step * N1 * s)
-                rr[0, r, s * classes : (s + 1) * classes, :] = p
-                rr[1, r, s * classes : (s + 1) * classes, :] = m
         norm = jnp.broadcast_to(jnp.sum(square, axis=1, keepdims=True), (classes, cols))
         k = lax.broadcasted_iota(jnp.int32, (classes, cols), 0)
         lane = lax.broadcasted_iota(jnp.int32, (classes, cols), 1)
         norm = jnp.sum(jnp.where(lane % classes == k, norm, 0.0), axis=0, keepdims=True)
         for i in range(2):
             left = jnp.concatenate([x_ref[i, r] for r in range(cycles)], axis=1)
-            right = jnp.concatenate([rr[i, r] for r in range(cycles)], axis=1)
+            right = []
+            for r in range(cycles):
+                v = take_cycle(scr, r, classes, cycles)[i].astype(BF)
+                v = [turn(v, v, angles - step * N1 * s)[i] for s in range(N2)]
+                right.append(jnp.concatenate(v, axis=0))
+            right = jnp.concatenate(right, axis=1)
             part = lax.dot_general(
                 left, right, (((1,), (1,)), ((), ())), preferred_element_type=F32
             )
@@ -206,10 +207,7 @@
         out_shape=VM((nb, tiles, 2 * rows, LANES), BF),
         in_specs=[spec()] * (len(refs) + tiles),
         out_specs=spec(),
-        scratch_shapes=[
-            VM((2, classes * cycles, LANES), F32),
-            VM((2, cycles, cols, LANES), BF),
-        ],
+        scratch_shapes=[VM((2, classes * cycles, LANES), F32)],
         compiler_params=params(),
         name="correlate",
     )(here(turned), *[here(r) for r in (*refs, *before)])

time: 62.4 us -> 62.3 us (level)
  Pallas kernels: 10 us -> 9.26 us
  transfers between devices with their start and end apart: 7 -> 7, of which waited for: 2 -> 3; matrix products, arithmetic and copies ran while one was open for 0% -> 0% of each run, Pallas kernels for 9% -> 8%
where the time goes in v1:
time: 62.3 us; the launch traced here: 62.1 us
  blocking collectives  39.6 us (64%)
  starting transfers between devices  9.28 us (15%)
  Pallas kernels  9.26 us (15%)
  waiting for transfers between devices  3.82 us (6%)
    all_to_all x1, blocking collectives, shards(): scores = lax.all_to_all(scores, 'blk', 0, 0)  13.4 us
    all_to_all x1, blocking collectives, shards(): totals = lax.all_to_all(totals, ('yh', 'z'), 0, 0)  13.2 us
    all_to_all x1, blocking collectives, shards(): weights = lax.all_to_all(weights, 'blk', 0, 0)  12.9 us
    ppermute x3, starting transfers between devices, shards(): refs.append(lax.ppermute(refs[0], 'z', ring))  5.61 us
    ppermute x1, starting transfers between devices, shards(): theirs = lax.ppermute(mine, 'yh', swap)  3.39 us
    pallas_call x2, Pallas kernels, correlate(): pl.pallas_call(body, out_shape=VM((nb, tiles, 2 * rows, LANES), BF), in_s...  2.67 us
    ppermute x3, waiting for transfers between devices, shards(): refs.append(lax.ppermute(refs[0], 'z', ring))  2.46 us
    pallas_call x1, Pallas kernels, halve_images(): pl.pallas_call(body, out_shape=VM((2, cycles, 2 * particles, LANES), BF),...  1.68 us
  transfers between devices with their start and end apart: 7, of which 3 were waited for; matrix products, arithmetic and copies ran while one was open for 0% of the time, Pallas kernels for 8%

profile of v1, /device:TPU:0, one launch (start us, length us, event | category | flops | bytes accessed | tf_op | source)
XLA Modules:
  0.0 62.1 jit_solution(9972049439593134170)
XLA Ops:
  0.0 0.0 collective-permute-start
  0.0 1.2 %pick_block.1.a_ref = bf16[64,256]{1,0:T(8,128)(2,1)S(1)} custom-call(s32[1]{0:T(128)} %bitcast.me_ref, s32[16]{0:T(128)} %owner_ref.1, f32[64]{0:T(128)} %gain_ref.1, bf16[16,4,16,256]{3,2,1,0:T(8,128)(2,1)} %bitcast.7), custom_call_target="tpu_custom_call" | custom-call | tf_op jit(solution)/shard_map/pick_block/pallas_call | solution.py:79
  1.2 3.4 %collective-permute-start.1 = (bf16[64,256]{1,0:T(8,128)(2,1)S(1)}, bf16[64,256]{1,0:T(8,128)(2,1)S(1)}, u32[]{:S(2)}, u32[]{:S(2)}) collective-permute-start(bf16[64,256]{1,0:T(8,128)(2,1)S(1)} %pick_block.1.a_ref), channel_id=1, source_target_pairs={{0,64},{64,0},{1,65},{65,1},{2,66},{66,2},{3,67},{67,3},{4,68},{68... | collective-permute-start | bytes 98312 | tf_op jit(solution)/shard_map/ppermute | solution.py:385
  4.6 0.2 collective-permute-start.2
  4.8 0.0 collective-permute-done.other_ref
  4.8 1.7 %halve_images.1.x_ref.refs_0_ = bf16[2,16,128,128]{3,2,1,0:T(8,128)(2,1)S(1)} custom-call(bf16[64,16,256]{2,1,0:T(8,128)(2,1)} %own_hbm.1, bf16[64,16,256]{2,1,0:T(8,128)(2,1)S(1)} %collective-permute-done.other_ref), custom_call_target="tpu_custom_call" | custom-call | tf_op jit(solution)/shard_map/halve_images/pallas_call | solution.py:109
  6.5 0.0 collective-permute-done.2.refs_1_
  6.5 0.2 collective-permute-done.1.b_ref
  6.7 2.0 %collective-permute-start.5 = (bf16[2,64,256]{2,1,0:T(8,128)(2,1)S(1)}, bf16[2,64,256]{2,1,0:T(8,128)(2,1)S(1)}, u32[]{:S(2)}, u32[]{:S(2)}) collective-permute-start(bf16[2,64,256]{2,1,0:T(8,128)(2,1)S(1)} %pair_up.1.args_0_), channel_id=1, source_target_pairs={{0,16},{16,0},{32,48},{48,32},{1,17},{17,1},{33,49},{49,33},{2,18}... | collective-permute-start | bytes 196616 | tf_op jit(solution)/shard_map/ppermute | solution.py:390
  8.7 2.5 %collective-permute-start.3 = (bf16[2,64,256]{2,1,0:T(8,128)(2,1)S(1)}, bf16[2,64,256]{2,1,0:T(8,128)(2,1)S(1)}, u32[]{:S(2)}, u32[]{:S(2)}) collective-permute-start(bf16[2,64,256]{2,1,0:T(8,128)(2,1)S(1)} %pair_up.1.args_0_), channel_id=1, source_target_pairs={{0,48},{16,32},{32,16},{48,0},{1,49},{17,33},{33,17},{49,1},{2,50}... | collective-permute-start | bytes 196616 | tf_op jit(solution)/shard_map/ppermute | solution.py:390
  11.2 1.1 %collective-permute-start.4 = (bf16[2,64,256]{2,1,0:T(8,128)(2,1)S(1)}, bf16[2,64,256]{2,1,0:T(8,128)(2,1)S(1)}, u32[]{:S(2)}, u32[]{:S(2)}) collective-permute-start(bf16[2,64,256]{2,1,0:T(8,128)(2,1)S(1)} %pair_up.1.args_0_), channel_id=1, source_target_pairs={{0,32},{16,48},{32,0},{48,16},{1,33},{17,49},{33,1},{49,17},{2,34}... | collective-permute-start | bytes 196616 | tf_op jit(solution)/shard_map/ppermute | solution.py:390
  12.3 0.9 %turn_images.1.x_ref = bf16[2,16,512,128]{3,2,1,0:T(8,128)(2,1)S(1)} custom-call(bf16[2,16,128,128]{3,2,1,0:T(8,128)(2,1)S(1)} %halve_images.1.x_ref.refs_0_), custom_call_target="tpu_custom_call" | custom-call | tf_op jit(solution)/shard_map/turn_images/pallas_call | solution.py:156
  13.2 0.0 collective-permute-done.5.args_1_
  13.2 1.3 %correlate.2.args_2_ = bf16[8,1,128,128]{3,2,1,0:T(8,128)(2,1)S(1)} custom-call(bf16[2,16,512,128]{3,2,1,0:T(8,128)(2,1)S(1)} %turn_images.1.x_ref, bf16[2,64,256]{2,1,0:T(8,128)(2,1)S(1)} %pair_up.1.args_0_, bf16[2,64,256]{2,1,0:T(8,128)(2,1)S(1)} %collective-permute-done.5.args_1_), custom_call_target="tpu_custom_call" | custom-call | tf_op jit(solution)/shard_map/correlate/pallas_call | solution.py:205
  14.5 0.0 copy-start
  14.5 0.0 collective-permute-done.3.args_0_
  14.6 2.5 %collective-permute-done.4.args_1_ = bf16[2,64,256]{2,1,0:T(8,128)(2,1)S(1)} collective-permute-done((bf16[2,64,256]{2,1,0:T(8,128)(2,1)S(1)}, bf16[2,64,256]{2,1,0:T(8,128)(2,1)S(1)}, u32[]{:S(2)}, u32[]{:S(2)}) %collective-permute-start.4) | collective-permute-done | bytes 65568 | tf_op jit(solution)/shard_map/ppermute | solution.py:390
  17.0 1.3 %correlate.3 = bf16[8,2,128,128]{3,2,1,0:T(8,128)(2,1)S(1)} custom-call(bf16[2,16,512,128]{3,2,1,0:T(8,128)(2,1)S(1)} %turn_images.1.x_ref, bf16[2,64,256]{2,1,0:T(8,128)(2,1)S(1)} %collective-permute-done.3.args_0_, bf16[2,64,256]{2,1,0:T(8,128)(2,1)S(1)} %collective-permute-done.4.args_1_, bf16[8,1,128,128]{3,2,1,0:T(8,128)(2,1)S(1)} %correlate.2.args_2_), custom_call_target="tpu_custom_call" | custom-call | tf_op jit(solution)/shard_map/correlate/pallas_call | solution.py:205
  18.3 13.4 %all_to_all.15.x_ref = bf16[8,2,128,128]{3,2,1,0:T(8,128)(2,1)S(1)} all-to-all(bf16[8,2,128,128]{3,2,1,0:T(8,128)(2,1)S(1)} %correlate.3), channel_id=1, replica_groups=mesh['yh'=2,'z'=4,'core'=2,'blk'=8] {'blk'}, dimensions={0} | all-to-all | bytes 1048576 | tf_op jit(solution)/shard_map/all_to_all | solution.py:394
  31.8 0.0 copy-done
  31.8 0.4 local_softmax.1
  32.2 0.1 collective-permute-start.6
  32.3 1.2 %collective-permute-done.6.b_ref = f32[2,16,128]{2,1,0:T(8,128)S(1)} collective-permute-done((f32[2,16,128]{2,1,0:T(8,128)S(1)}, f32[2,16,128]{2,1,0:T(8,128)S(1)}, u32[]{:S(2)}, u32[]{:S(2)}) %collective-permute-start.6) | collective-permute-done | bytes 16416 | tf_op jit(solution)/shard_map/ppermute | solution.py:399
  33.4 0.1 normalize.1
  33.6 12.9 %all_to_all.16.w_ref = bf16[8,256,128]{2,1,0:T(8,128)(2,1)S(1)} all-to-all(bf16[8,256,128]{2,1,0:T(8,128)(2,1)S(1)} %normalize.1), channel_id=1, replica_groups=mesh['yh'=2,'z'=4,'core'=2,'blk'=8] {'blk'}, dimensions={0} | all-to-all | bytes 1048576 | tf_op jit(solution)/shard_map/all_to_all | solution.py:401
  46.5 1.6 %accumulate.1 = bf16[8,64,256]{2,1,0:T(8,128)(2,1)S(1)} custom-call(s32[1]{0:T(128)} %bitcast.me_ref, bf16[8,256,128]{2,1,0:T(8,128)(2,1)S(1)} %all_to_all.16.w_ref, bf16[2,16,512,128]{3,2,1,0:T(8,128)(2,1)S(1)} %turn_images.1.x_ref), custom_call_target="tpu_custom_call" | custom-call | tf_op jit(solution)/shard_map/accumulate/pallas_call | solution.py:339
  48.2 13.2 %all_to_all.17.x_ref = bf16[8,64,256]{2,1,0:T(8,128)(2,1)S(1)} all-to-all(bf16[8,64,256]{2,1,0:T(8,128)(2,1)S(1)} %accumulate.1), channel_id=1, replica_groups=mesh['yh'=2,'z'=4,'core'=2,'blk'=8] {'yh','z'}, dimensions={0} | all-to-all | bytes 524288 | tf_op jit(solution)/shard_map/all_to_all | solution.py:403
  61.4 0.7 %add_up.1 = f32[64,256]{1,0:T(8,128)} custom-call(bf16[8,64,256]{2,1,0:T(8,128)(2,1)S(1)} %all_to_all.17.x_ref), custom_call_target="tpu_custom_call" | custom-call | tf_op jit(solution)/shard_map/add_up/pallas_call | solution.py:359
  (1 shorter events, 0.0 us)
Async XLA Ops:
  0.0 4.8 %collective-permute-start = (bf16[64,16,256]{2,1,0:T(8,128)(2,1)}, bf16[64,16,256]{2,1,0:T(8,128)(2,1)S(1)}, u32[]{:S(2)}, u32[]{:S(2)}) collective-permute-start(bf16[64,16,256]{2,1,0:T(8,128)(2,1)} %own_hbm.1), channel_id=1, source_target_pairs={{0,8},{8,0},{1,9},{9,1},{2,10},{10,2},{3,11},{11,3},{4,12},{12,4},... | collective-permute-start | bytes 1572872 | tf_op jit(solution)/shard_map/ppermute | solution.py:379
  1.2 5.5 %collective-permute-start.1 = (bf16[64,256]{1,0:T(8,128)(2,1)S(1)}, bf16[64,256]{1,0:T(8,128)(2,1)S(1)}, u32[]{:S(2)}, u32[]{:S(2)}) collective-permute-start(bf16[64,256]{1,0:T(8,128)(2,1)S(1)} %pick_block.1.a_ref), channel_id=1, source_target_pairs={{0,64},{64,0},{1,65},{65,1},{2,66},{66,2},{3,67},{67,3},{4,68},{68... | collective-permute-start | bytes 98312 | tf_op jit(solution)/shard_map/ppermute | solution.py:385
  4.6 1.9 %collective-permute-start.2 = (f32[64]{0:T(128)}, f32[64]{0:T(128)S(1)}, u32[]{:S(2)}, u32[]{:S(2)}) collective-permute-start(f32[64]{0:T(128)} %param.9), channel_id=1, source_target_pairs={{0,8},{8,0},{1,9},{9,1},{2,10},{10,2},{3,11},{11,3},{4,12},{12,4},... | collective-permute-start | bytes 776 | tf_op jit(solution)/shard_map/ppermute | solution.py:380
  6.7 6.5 %collective-permute-start.5 = (bf16[2,64,256]{2,1,0:T(8,128)(2,1)S(1)}, bf16[2,64,256]{2,1,0:T(8,128)(2,1)S(1)}, u32[]{:S(2)}, u32[]{:S(2)}) collective-permute-start(bf16[2,64,256]{2,1,0:T(8,128)(2,1)S(1)} %pair_up.1.args_0_), channel_id=1, source_target_pairs={{0,16},{16,0},{32,48},{48,32},{1,17},{17,1},{33,49},{49,33},{2,18}... | collective-permute-start | bytes 196616 | tf_op jit(solution)/shard_map/ppermute | solution.py:390
  8.7 5.8 %collective-permute-start.3 = (bf16[2,64,256]{2,1,0:T(8,128)(2,1)S(1)}, bf16[2,64,256]{2,1,0:T(8,128)(2,1)S(1)}, u32[]{:S(2)}, u32[]{:S(2)}) collective-permute-start(bf16[2,64,256]{2,1,0:T(8,128)(2,1)S(1)} %pair_up.1.args_0_), channel_id=1, source_target_pairs={{0,48},{16,32},{32,16},{48,0},{1,49},{17,33},{33,17},{49,1},{2,50}... | collective-permute-start | bytes 196616 | tf_op jit(solution)/shard_map/ppermute | solution.py:390
  11.2 5.8 %collective-permute-start.4 = (bf16[2,64,256]{2,1,0:T(8,128)(2,1)S(1)}, bf16[2,64,256]{2,1,0:T(8,128)(2,1)S(1)}, u32[]{:S(2)}, u32[]{:S(2)}) collective-permute-start(bf16[2,64,256]{2,1,0:T(8,128)(2,1)S(1)} %pair_up.1.args_0_), channel_id=1, source_target_pairs={{0,32},{16,48},{32,0},{48,16},{1,33},{17,49},{33,1},{49,17},{2,34}... | collective-permute-start | bytes 196616 | tf_op jit(solution)/shard_map/ppermute | solution.py:390
  14.5 17.3 %copy-start = (f32[64]{0:T(128)S(1)}, f32[64]{0:T(128)}, u32[]{:S(2)}) copy-start(f32[64]{0:T(128)} %param.9) | copy-start | bytes 772
  32.2 1.2 %collective-permute-start.6 = (f32[2,16,128]{2,1,0:T(8,128)S(1)}, f32[2,16,128]{2,1,0:T(8,128)S(1)}, u32[]{:S(2)}, u32[]{:S(2)}) collective-permute-start(f32[2,16,128]{2,1,0:T(8,128)S(1)} %get-tuple-element.8.a_ref), channel_id=1, source_target_pairs={{0,8},{8,0},{1,9},{9,1},{2,10},{10,2},{3,11},{11,3},{4,12},{12,4},... | collective-permute-start | bytes 49160 | tf_op jit(solution)/shard_map/ppermute | solution.py:399
